TPU v7x, 256 devices: a whole 4x4x8 slice. The times are simulated.
256 devices in a mesh: ctx: 64 (over y, z, x_hi), tp: 4 (over x_lo, core).
Axes of the slice: x: 4 (x_hi: 2, x_lo: 2; x = x_hi * 2 + x_lo), y: 4, z: 8, core: 2. Of those that a mesh axis runs over, the one named last changes fastest.
Arguments:
- queries: bfloat16 [4096, 3584], P('ctx', 'tp'), may hold values from -6 to 6
- keys: bfloat16 [4096, 512], P('ctx', 'tp'), may hold values from -5 to 5
- values: bfloat16 [4096, 512], P('ctx', 'tp'), may hold values from -6 to 6
- block_table: int32 [64], replicated, may hold values from 0 to 63, each once
- residual: bfloat16 [4096, 3584], P(('ctx', 'tp')), may hold values from -6 to 6
- out_weight: bfloat16 [3584, 3584], P('tp'), may hold values from -0.5 to 0.5
- norm_gain: bfloat16 [3584], replicated, may hold values from 0.099609375 to 1.8984375
- gate_logit_weight: bfloat16 [3584], replicated, may hold values from -0.09375 to 0.09375
- gate_weight: bfloat16 [3584, 20480], P(None, 'ctx'), may hold values from -0.09375 to 0.09375
- up_weight: bfloat16 [3584, 20480], P(None, 'ctx'), may hold values from -0.09375 to 0.09375
- down_weight: bfloat16 [20480, 3584], P('ctx'), may hold values from -0.0390625 to 0.0390625
Outputs:
- layer_out: bfloat16 [4096, 3584], P(('ctx', 'tp'))
Inputs may be any that keep to these rules, and one draw needn't show every extreme that they name: Each entry names a different pair; slot c holds blocks block_table[c] and its mirror, counted from the end of the prompt.
All inputs are finite; a program needn't handle non-finite values.
Results may differ from a plain program's by a relative error of at most 0.017.
Values may be sent and summed in bfloat16 or wider, within the bound.
No kernel may reach another device: no remote copies, remote signals or barrier semaphores. Data moves between devices by JAX's collectives and lax.ppermute only.
A program may use at most 128 MiB of HBM per device.

v0:
```python
import jax
import jax.numpy as jnp
from jax import lax
from jax.sharding import PartitionSpec as P

HEADS = 28
KV_HEADS = 4
HEAD_DIM = 128


def per_device(
    queries,
    keys,
    values,
    block_table,
    residual,
    out_weight,
    norm_gain,
    gate_logit_weight,
    gate_weight,
    up_weight,
    down_weight,
):
    tokens = queries.shape[0]
    half = tokens // 2
    ctx_count = lax.axis_size("ctx")
    tp_count = lax.axis_size("tp")
    quarter = tokens // tp_count
    group = HEADS // KV_HEADS
    kv_local = keys.shape[1] // HEAD_DIM
    scale = HEAD_DIM ** (-0.5)
    mirror = 2 * ctx_count - 1
    slots = jnp.arange(ctx_count, dtype=jnp.int32)

    def row_positions(first_row, count):
        rows = first_row + jnp.arange(count, dtype=jnp.int32)
        owner = rows // tokens
        local = rows % tokens
        onehot = (owner[:, None] == slots[None, :]).astype(jnp.int32)
        pair = jnp.sum(onehot * block_table[None, :], axis=1)
        return jnp.where(local < half, pair * half + local, (mirror - pair) * half + local - half)

    own_place = row_positions(lax.axis_index("ctx") * tokens, tokens)
    query_heads = queries.reshape(tokens, kv_local, group, HEAD_DIM)
    start_max = jnp.full((kv_local, group, tokens), -1e30, jnp.float32)
    key_piece = lax.all_gather(keys, "ctx", axis=0, tiled=True)
    value_piece = lax.all_gather(values, "ctx", axis=0, tiled=True)
    count = key_piece.shape[0]
    key_place = row_positions(jnp.int32(0), count)
    key_heads = key_piece.reshape(count, kv_local, HEAD_DIM)
    value_heads = value_piece.reshape(count, kv_local, HEAD_DIM)
    score = (
        jnp.einsum("tkgd,pkd->kgtp", query_heads, key_heads, preferred_element_type=jnp.float32)
        * scale
    )
    visible = key_place[None, :] <= own_place[:, None]
    score = jnp.where(visible, score, -1e30)
    new_max = jnp.maximum(start_max, jnp.max(score, axis=-1))
    weight = jnp.where(visible, jnp.exp(score - new_max[..., None]), 0.0)
    new_sum = jnp.sum(weight, axis=-1)
    added = jnp.einsum(
        "kgtp,pkd->kgtd",
        weight.astype(jnp.bfloat16),
        value_heads,
        preferred_element_type=jnp.float32,
    )
    summed = added / new_sum[..., None]
    attended_heads = (
        jnp.transpose(summed, (2, 0, 1, 3))
        .astype(jnp.bfloat16)
        .reshape(tokens, kv_local * group * HEAD_DIM)
    )
    projected = jnp.dot(attended_heads, out_weight, preferred_element_type=jnp.float32)
    total = lax.psum(projected.astype(jnp.bfloat16), "tp").astype(jnp.float32)
    head_sum = lax.dynamic_slice_in_dim(total, lax.axis_index("tp") * quarter, quarter, 0)
    attended = (residual.astype(jnp.float32) + head_sum).astype(jnp.bfloat16)
    attended = lax.optimization_barrier(attended)
    attended_f = attended.astype(jnp.float32)
    mean_square = jnp.mean(attended_f * attended_f, axis=-1, keepdims=True)
    normed = (attended_f * lax.rsqrt(mean_square + 1e-06) * norm_gain.astype(jnp.float32)).astype(
        jnp.bfloat16
    )
    gate_prob = jax.nn.sigmoid(
        jnp.dot(normed, gate_logit_weight, preferred_element_type=jnp.float32)
    )
    piece = lax.all_gather(normed, "ctx", axis=0, tiled=True)
    gate_part = jnp.dot(piece, gate_weight, preferred_element_type=jnp.float32)
    up_part = jnp.dot(piece, up_weight, preferred_element_type=jnp.float32)
    hidden = (jax.nn.silu(gate_part) * up_part).astype(jnp.bfloat16)
    rows = hidden
    shared = lax.psum_scatter(
        jnp.dot(rows, down_weight, preferred_element_type=jnp.float32),
        "ctx",
        scatter_dimension=0,
        tiled=True,
    )
    return (attended_f + gate_prob[:, None] * shared).astype(jnp.bfloat16)


def solution(mesh):
    return jax.shard_map(
        per_device,
        mesh=mesh,
        in_specs=(
            P("ctx", "tp"),
            P("ctx", "tp"),
            P("ctx", "tp"),
            P(),
            P(("ctx", "tp"), None),
            P("tp", None),
            P(),
            P(),
            P(None, "ctx"),
            P(None, "ctx"),
            P("ctx", None),
        ),
        out_specs=P(("ctx", "tp"), None),
        check_vma=False,
    )
```

profile of v0, /device:TPU:0, one launch (start us, length us, event | category | flops | bytes accessed | tf_op | source)
XLA Modules:
  0.0 864.5 jit_solution(11348240395880294920)
XLA Ops:
  6.5 0.0 copy-start
  6.5 0.0 all-gather.4.cloned.1.call-start
  6.5 0.7 all-gather.4.cloned.1.call-update
  7.3 0.0 all-gather.6.cloned.1.call-start
  7.3 0.7 all-gather.6.cloned.1.call-update
  8.0 0.0 all-reduce.2.cloned.1.call-start
  8.1 0.8 select_reduce_fusion.1
  8.9 0.9 select_reduce_fusion
  9.9 0.2 broadcast_compare_fusion
  10.1 116.2 %all-gather.4.cloned.1.call-done = bf16[4096,128]{1,0:T(8,128)(2,1)} async-done(((bf16[64,128]{1,0:T(8,128)(2,1)}), bf16[4096,128]{1,0:T(8,128)(2,1)}) %all-gather.4.cloned.1.call-update) | async-done | bytes 1048592 | tf_op jit(solution)/shard_map/all_gather | solution.py:46
  126.3 2.7 fusion
  129.0 0.0 copy-start.1
  129.0 2.9 copy-done.1
  131.9 2.2 fusion.1
  134.1 106.7 %all-gather.6.cloned.1.call-done = bf16[4096,128]{1,0:T(8,128)(2,1)} async-done(((bf16[64,128]{1,0:T(8,128)(2,1)}), bf16[4096,128]{1,0:T(8,128)(2,1)}) %all-gather.6.cloned.1.call-update) | async-done | bytes 1048592 | tf_op jit(solution)/shard_map/all_gather | solution.py:47
  240.9 5.2 fusion.19
  246.0 0.0 copy-start.4
  246.0 0.0 copy-start.3
  246.1 0.1 copy.16
  246.1 4.8 convolution_convert_fusion
  251.0 0.0 all-reduce.2.cloned.1.call-update
  251.0 0.0 all-gather.8.cloned.1.call-start
  251.1 0.0 copy-done.4
  251.1 39.2 %all-reduce.2.cloned.1.call-done = bf16[64,3584]{1,0:T(8,128)(2,1)} async-done(((bf16[64,3584]{1,0:T(8,128)(2,1)}), bf16[64,3584]{1,0:T(8,128)(2,1)}) %all-reduce.2.cloned.1.call-update) | async-done | bytes 458768 | tf_op jit(solution)/shard_map/psum | solution.py:74
  290.3 0.0 copy-done.3
  290.3 0.9 add_convert_fusion
  291.3 0.1 fusion.26
  291.4 0.7 fusion.28
  292.2 0.0 all-gather.8.cloned.1.call-update
  292.2 0.2 reduce-scatter.2.cloned.1.call-start
  292.4 147.2 %all-gather.8.cloned.1.call-done = bf16[1024,3584]{1,0:T(8,128)(2,1)} async-done(((bf16[16,3584]{1,0:T(8,128)(2,1)}), bf16[1024,3584]{1,0:T(8,128)(2,1)}) %all-gather.8.cloned.1.call-update) | async-done | bytes 7340048 | tf_op jit(solution)/shard_map/all_gather | solution.py:86
  439.7 7.4 fusion.44
  447.1 0.0 copy-done
  447.1 12.9 %fusion.8 = f32[1024,3584]{1,0:T(8,128)} fusion(bf16[320,3584]{1,0:T(8,128)(2,1)S(1)} %copy-done, bf16[1024,3584]{1,0:T(8,128)(2,1)} %all-gather.8.cloned.1.call-done, bf16[3584,320]{0,1:T(8,128)(2,1)} %param.20, f32[1024,320]{0,1:T(8,128)} %fusion.44), kind=kOutput, calls=%fused_computation.11 | convolution fusion | flops 4699586560 | bytes 27918336 | tf_op jit(solution)/shard_map/dot_general | solution.py:92
  460.0 0.0 copy-start.5
  460.0 0.0 copy-start.2
  460.0 0.0 reduce-scatter.2.cloned.1.call-update
  460.0 0.7 copy-done.5
  460.7 0.2 copy-done.2
  460.9 0.1 fusion.12
  461.1 395.3 %reduce-scatter.2.cloned.1.call-done = f32[16,3584]{1,0:T(8,128)} async-done(((f32[1024,3584]{1,0:T(8,128)}), f32[16,3584]{1,0:T(8,128)}) %reduce-scatter.2.cloned.1.call-update) | async-done | bytes 229392 | tf_op jit(solution)/shard_map/reduce_scatter | solution.py:91
  856.3 1.7 fusion.29
  (8 shorter events, 0.1 us)
Async XLA Ops:
  6.5 440.5 %copy-start = (bf16[320,3584]{1,0:T(8,128)(2,1)S(1)}, bf16[320,3584]{1,0:T(8,128)(2,1)}, u32[]{:S(2)}) copy-start(bf16[320,3584]{1,0:T(8,128)(2,1)} %param.21) | copy-start | bytes 6881284
  6.5 119.8 %all-gather.4.cloned.1.call-start = ((), (), s32[]{:S(2)}) async-start(), calls=%async_computation.1 | async-start | bytes 1064960 | tf_op jit(solution)/shard_map/all_gather | solution.py:46
  7.3 233.6 %all-gather.6.cloned.1.call-start = ((), (), s32[]{:S(2)}) async-start(), calls=%async_computation.2 | async-start | bytes 1064960 | tf_op jit(solution)/shard_map/all_gather | solution.py:47
  8.0 282.3 %all-reduce.2.cloned.1.call-start = ((), (), s32[]{:S(2)}) async-start(), calls=%async_computation.3 | async-start | bytes 917504 | tf_op jit(solution)/shard_map/psum | solution.py:74
  129.0 3.0 copy-start.1
  246.0 5.0 copy-start.4
  246.0 44.3 %copy-start.3 = (bf16[16,3584]{1,0:T(8,128)(2,1)S(1)}, bf16[16,3584]{1,0:T(8,128)(2,1)}, u32[]{:S(2)}) copy-start(bf16[16,3584]{1,0:T(8,128)(2,1)} %param.15) | copy-start | bytes 344068
  251.0 188.6 %all-gather.8.cloned.1.call-start = ((), (), s32[]{:S(2)}) async-start(), calls=%async_computation.4 | async-start | bytes 7454720 | tf_op jit(solution)/shard_map/all_gather | solution.py:86
  292.2 564.1 %reduce-scatter.2.cloned.1.call-start = ((), (), s32[]{:S(2)}) async-start(), calls=%async_computation.5 | async-start | bytes 14909440 | tf_op jit(solution)/shard_map/reduce_scatter | solution.py:91
  460.0 0.7 copy-start.5
  460.0 0.9 copy-start.2
Sparse Core Ops, SparseCore 0:
  10.9 115.3 all-gather.3
  129.8 111.0 all-gather.5
  251.1 39.1 all-reduce.1
  294.2 145.3 all-gather.7
  460.1 396.1 reduce-scatter.1
where the time goes:
time: 865 us
  waiting for transfers between devices  806 us (93%)
  matrix products  33.1 us (4%)
  between operations  13.3 us (2%)
    reduce_scatter x1, waiting for transfers between devices, per_device(): lax.psum_scatter(jnp.dot(rows, down_weight, preferred_element_type=jnp.fl...  395 us
    all_gather x1, waiting for transfers between devices, per_device(): piece = lax.all_gather(normed, 'ctx', axis=0, tiled=True)  147 us
    all_gather x1, waiting for transfers between devices, per_device(): key_piece = lax.all_gather(keys, 'ctx', axis=0, tiled=True)  116 us
    all_gather x1, waiting for transfers between devices, per_device(): value_piece = lax.all_gather(values, 'ctx', axis=0, tiled=True)  107 us
    psum x1, waiting for transfers between devices, per_device(): total = lax.psum(projected.astype(jnp.bfloat16), 'tp').astype(jnp.float32)  39.2 us
  transfers between devices with their start and end apart: 5, of which 5 were waited for; matrix products, arithmetic and copies ran while one was open for 1% of the time, Pallas kernels for 0%

commit v1 on v0

--- a/solution.py
+++ b/solution.py
@@ -83,7 +83,12 @@
     gate_prob = jax.nn.sigmoid(
         jnp.dot(normed, gate_logit_weight, preferred_element_type=jnp.float32)
     )
-    piece = lax.all_gather(normed, "ctx", axis=0, tiled=True)
+    samples = []
+    for _ in range(lax.axis_size("ctx")):
+        samples.append(normed)
+    block_out = jnp.stack(samples)
+    kept_arr = lax.all_to_all(block_out, "ctx", 0, 0)
+    piece = jnp.concatenate(kept_arr, axis=0)
     gate_part = jnp.dot(piece, gate_weight, preferred_element_type=jnp.float32)
     up_part = jnp.dot(piece, up_weight, preferred_element_type=jnp.float32)
     hidden = (jax.nn.silu(gate_part) * up_part).astype(jnp.bfloat16)

time: 865 us -> 893 us (1.032)
  blocking collectives: 0 us -> 178 us
  waiting for transfers between devices: 806 us -> 655 us
    all_to_all x0 -> x1, blocking collectives: none -> 178 us  [per_device(): kept_arr = lax.all_to_all(block_out, 'ctx', 0, 0)]
    all_gather x1 -> x0, waiting for transfers between devices: 147 us -> none  [per_device(): piece = lax.all_gather(normed, 'ctx', axis=0, tiled=True)]
  transfers between devices with their start and end apart: 5 -> 4, of which waited for: 5 -> 4; matrix products, arithmetic and copies ran while one was open for 1% -> 1% of each run, Pallas kernels for 0% -> 0%
where the time goes in v1:
time: 893 us; the launch traced here: 891 us
  waiting for transfers between devices  655 us (73%)
  blocking collectives  178 us (20%)
  matrix products  29.4 us (3%)
  between operations  13.3 us (1%)
    reduce_scatter x1, waiting for transfers between devices, per_device(): lax.psum_scatter(jnp.dot(rows, down_weight, preferred_element_type=jnp.fl...  391 us
    all_to_all x1, blocking collectives, per_device(): kept_arr = lax.all_to_all(block_out, 'ctx', 0, 0)  178 us
    all_gather x1, waiting for transfers between devices, per_device(): key_piece = lax.all_gather(keys, 'ctx', axis=0, tiled=True)  116 us
    all_gather x1, waiting for transfers between devices, per_device(): value_piece = lax.all_gather(values, 'ctx', axis=0, tiled=True)  107 us
    psum x1, waiting for transfers between devices, per_device(): total = lax.psum(projected.astype(jnp.bfloat16), 'tp').astype(jnp.float32)  39.2 us
  transfers between devices with their start and end apart: 4, of which 4 were waited for; matrix products, arithmetic and copies ran while one was open for 1% of the time, Pallas kernels for 0%

profile of v1, /device:TPU:0, one launch (start us, length us, event | category | flops | bytes accessed | tf_op | source)
XLA Modules:
  0.0 890.7 jit_solution(18384159389226386558)
XLA Ops:
  6.5 0.0 copy-start
  6.5 0.0 all-gather.3.cloned.1.call-start
  6.5 0.7 all-gather.3.cloned.1.call-update
  7.3 0.0 all-gather.5.cloned.1.call-start
  7.3 0.7 all-gather.5.cloned.1.call-update
  8.0 0.0 all-reduce.2.cloned.1.call-start
  8.1 0.8 select_reduce_fusion.1
  8.9 0.9 select_reduce_fusion
  9.9 0.2 broadcast_compare_fusion
  10.1 116.2 %all-gather.3.cloned.1.call-done = bf16[4096,128]{1,0:T(8,128)(2,1)} async-done(((bf16[64,128]{1,0:T(8,128)(2,1)}), bf16[4096,128]{1,0:T(8,128)(2,1)}) %all-gather.3.cloned.1.call-update) | async-done | bytes 1048592 | tf_op jit(solution)/shard_map/all_gather | solution.py:46
  126.3 2.7 fusion
  129.0 0.0 copy-start.2
  129.0 3.0 copy-done.2
  131.9 2.2 fusion.1
  134.1 106.7 %all-gather.5.cloned.1.call-done = bf16[4096,128]{1,0:T(8,128)(2,1)} async-done(((bf16[64,128]{1,0:T(8,128)(2,1)}), bf16[4096,128]{1,0:T(8,128)(2,1)}) %all-gather.5.cloned.1.call-update) | async-done | bytes 1048592 | tf_op jit(solution)/shard_map/all_gather | solution.py:47
  240.9 5.2 fusion.19
  246.0 0.0 copy-start.4
  246.0 0.0 copy-start.3
  246.1 0.1 copy.16
  246.1 4.9 convolution_convert_fusion
  251.0 0.0 all-reduce.2.cloned.1.call-update
  251.0 0.0 reduce-scatter.2.cloned.1.call-start
  251.1 0.0 copy-done.4
  251.1 39.2 %all-reduce.2.cloned.1.call-done = bf16[64,3584]{1,0:T(8,128)(2,1)} async-done(((bf16[64,3584]{1,0:T(8,128)(2,1)}), bf16[64,3584]{1,0:T(8,128)(2,1)}) %all-reduce.2.cloned.1.call-update) | async-done | bytes 458768 | tf_op jit(solution)/shard_map/psum | solution.py:74
  290.3 0.0 copy-done.3
  290.3 0.9 add_convert_fusion
  291.3 0.1 fusion.26
  291.4 0.1 fusion.28
  291.5 0.9 stack.2
  292.4 0.0 copy-start.6
  292.4 178.4 %all_to_all.5 = bf16[64,16,3584]{2,1,0:T(8,128)(2,1)S(1)} all-to-all(bf16[64,16,3584]{2,1,0:T(8,128)(2,1)S(1)} %stack.2), channel_id=1, replica_groups=mesh['ctx'=64,'tp'=4] {'ctx'}, dimensions={0} | all-to-all | bytes 14680064 | tf_op jit(solution)/shard_map/all_to_all | solution.py:90
  470.8 0.0 copy-start.1
  470.8 2.9 copy-done.1
  473.7 0.0 copy-done.6
  473.7 3.7 fusion.44
  477.4 0.0 copy-done
  477.4 12.9 %fusion.8 = f32[1024,3584]{1,0:T(8,128)} fusion(bf16[320,3584]{1,0:T(8,128)(2,1)S(1)} %copy-done, bf16[1024,3584]{1,0:T(8,128)(2,1)} %bitcast.77, bf16[3584,320]{0,1:T(8,128)(2,1)} %param.20, f32[1024,320]{0,1:T(8,128)} %fusion.44), kind=kOutput, calls=%fused_computation.11 | convolution fusion | flops 4699586560 | bytes 27918336 | tf_op jit(solution)/shard_map/dot_general | solution.py:97
  490.3 0.0 copy-start.5
  490.3 0.0 reduce-scatter.2.cloned.1.call-update
  490.4 0.7 copy-done.5
  491.0 0.1 fusion.12
  491.2 391.3 %reduce-scatter.2.cloned.1.call-done = f32[16,3584]{1,0:T(8,128)} async-done(((f32[1024,3584]{1,0:T(8,128)}), f32[16,3584]{1,0:T(8,128)}) %reduce-scatter.2.cloned.1.call-update) | async-done | bytes 229392 | tf_op jit(solution)/shard_map/reduce_scatter | solution.py:96
  882.5 1.7 fusion.29
  (8 shorter events, 0.1 us)
Async XLA Ops:
  6.5 470.9 %copy-start = (bf16[320,3584]{1,0:T(8,128)(2,1)S(1)}, bf16[320,3584]{1,0:T(8,128)(2,1)}, u32[]{:S(2)}) copy-start(bf16[320,3584]{1,0:T(8,128)(2,1)} %param.21) | copy-start | bytes 6881284
  6.5 119.8 %all-gather.3.cloned.1.call-start = ((), (), s32[]{:S(2)}) async-start(), calls=%async_computation.2 | async-start | bytes 1064960 | tf_op jit(solution)/shard_map/all_gather | solution.py:46
  7.3 233.6 %all-gather.5.cloned.1.call-start = ((), (), s32[]{:S(2)}) async-start(), calls=%async_computation.3 | async-start | bytes 1064960 | tf_op jit(solution)/shard_map/all_gather | solution.py:47
  8.0 282.3 %all-reduce.2.cloned.1.call-start = ((), (), s32[]{:S(2)}) async-start(), calls=%async_computation.4 | async-start | bytes 917504 | tf_op jit(solution)/shard_map/psum | solution.py:74
  129.0 3.0 copy-start.2
  246.0 5.0 copy-start.4
  246.0 44.3 %copy-start.3 = (bf16[16,3584]{1,0:T(8,128)(2,1)S(1)}, bf16[16,3584]{1,0:T(8,128)(2,1)}, u32[]{:S(2)}) copy-start(bf16[16,3584]{1,0:T(8,128)(2,1)} %param.15) | copy-start | bytes 344068
  251.0 631.5 %reduce-scatter.2.cloned.1.call-start = ((), (), s32[]{:S(2)}) async-start(), calls=%async_computation.5 | async-start | bytes 14909440 | tf_op jit(solution)/shard_map/reduce_scatter | solution.py:96
  292.4 181.3 %copy-start.6 = (bf16[3584,320]{0,1:T(8,128)(2,1)S(1)}, bf16[3584,320]{0,1:T(8,128)(2,1)}, u32[]{:S(2)}) copy-start(bf16[3584,320]{0,1:T(8,128)(2,1)} %param.19) | copy-start | bytes 6881284
  470.8 2.9 copy-start.1
  490.3 0.7 copy-start.5
Sparse Core Ops, SparseCore 0:
  10.9 115.3 all-gather.2
  129.8 111.0 all-gather.4
  251.1 39.1 all-reduce.1
  490.5 391.9 reduce-scatter.1
